TPU v7x, 512 devices: a whole 4x8x8 slice. The times are simulated.
512 devices in a mesh: dp: 32 (over x, y), segment: 2 (over core), mp: 8 (over z).
Axes of the slice: x: 4, y: 8, z: 8, core: 2. Of those that a mesh axis runs over, the one named last changes fastest.
Arguments:
- frames: bfloat16 [2, 8192, 1280], P(None, ('dp', 'mp')), may hold values from -8 to 8
- dec_states: bfloat16 [2, 2048, 1280], P(None, 'dp'), may hold values from -8 to 8
- out_grad: bfloat16 [2, 2048, 1280], P(None, 'dp'), may hold values from -3 to 3
- frame_lengths: int32 [2, 32, 4], P(None, 'dp'), may hold values from 1 to 128, 256 in all within a row
- token_lengths: int32 [2, 32, 4], P(None, 'dp'), may hold values from 1 to 32, 64 in all within a row
- weights: bfloat16 [2, 4, 1024, 1280], P('segment', None, 'mp'), may hold values from -1 to 1
- norm_gains: float32 [3, 1280], replicated, may hold values from 0.25 to 1.75
- norm_biases: float32 [3, 1280], replicated, may hold values from -2 to 2
Outputs:
- gradient: float32 [2, 3, 1024, 1280], P('segment', None, 'mp')
Inputs may be any that keep to these rules, and one draw needn't show every extreme that they name: `frame_lengths`: the 4 utterance lengths of each micro-batch and group sum to 256. `token_lengths`: the 4 token counts of each micro-batch and group sum to 64.
All inputs are finite; a program needn't handle non-finite values.
Results may differ from a plain program's by a relative error of at most 0.04.
Values may be sent and summed in bfloat16 or wider, within the bound.
No kernel may reach another device: no remote copies, remote signals or barrier semaphores. Data moves between devices by JAX's collectives and lax.ppermute only.
A program may use at most 64 MiB of HBM per device.

v0:
```python
import math
import jax
import jax.numpy as jnp
from jax import lax
from jax.sharding import PartitionSpec as P

HS = 64
EPSILON = 1e-05
ROWS_DIMS = (((0,), (0,)), ((), ()))
FEAT_DIMS = (((1,), (1,)), ((), ()))


def layer_norm(values, norm_gain, offset):
    center = values - jnp.mean(values, axis=-1, keepdims=True)
    variance = jnp.mean(center * center, axis=-1, keepdims=True)
    return center * lax.rsqrt(variance + EPSILON) * norm_gain + offset


def norm_backward(grad_out, values, norm_gain):
    center = values - jnp.mean(values, axis=-1, keepdims=True)
    variance = jnp.mean(center * center, axis=-1, keepdims=True)
    inverse = lax.rsqrt(variance + EPSILON)
    normed = center * inverse
    scaled = grad_out * norm_gain
    return inverse * (
        scaled
        - jnp.mean(scaled, axis=-1, keepdims=True)
        - normed * jnp.mean(scaled * normed, axis=-1, keepdims=True)
    )


def utterance_ids(lengths, row_count):
    bounds = jnp.cumsum(lengths, dtype=jnp.int32)
    places = jnp.arange(row_count, dtype=jnp.int32)
    return jnp.sum((places[:, None] >= bounds[None, :]).astype(jnp.int32), axis=1)


def project(row_block, matrix):
    return lax.dot_general(row_block, matrix, FEAT_DIMS, preferred_element_type=jnp.float32).astype(
        jnp.bfloat16
    )


def outer_rows(left_rows, right_rows):
    return lax.dot_general(left_rows, right_rows, ROWS_DIMS, preferred_element_type=jnp.float32)


def split_heads(row_block):
    return row_block.reshape(row_block.shape[0], -1, HS)


def attend(queries, key_rows, value_rows, allowed):
    scaling = 1.0 / math.sqrt(HS)
    scores = (
        jnp.einsum(
            "qhd,khd->hqk",
            split_heads(queries),
            split_heads(key_rows),
            preferred_element_type=jnp.float32,
        )
        * scaling
    )
    scores = jnp.where(allowed[None], scores, -1e30)
    highest = jnp.max(scores, axis=-1, keepdims=True)
    raised = jnp.exp(scores - highest)
    attn_probs = raised / jnp.sum(raised, axis=-1, keepdims=True)
    context = jnp.einsum(
        "hqk,khd->qhd",
        attn_probs.astype(jnp.bfloat16),
        split_heads(value_rows),
        preferred_element_type=jnp.float32,
    )
    return (context.reshape(queries.shape[0], -1).astype(jnp.bfloat16), attn_probs)


def attend_backward(queries, key_rows, value_rows, attn_probs, grad_context):
    scaling = 1.0 / math.sqrt(HS)
    grad_heads = split_heads(grad_context)
    grad_probs = jnp.einsum(
        "qhd,khd->hqk", grad_heads, split_heads(value_rows), preferred_element_type=jnp.float32
    )
    grad_scores = (
        attn_probs * (grad_probs - jnp.sum(grad_probs * attn_probs, axis=-1, keepdims=True))
    ).astype(jnp.bfloat16)
    key_grad = (
        jnp.einsum(
            "hqk,qhd->khd", grad_scores, split_heads(queries), preferred_element_type=jnp.float32
        )
        * scaling
    )
    key_grad = key_grad.reshape(key_rows.shape[0], -1).astype(jnp.bfloat16)
    value_grad = jnp.einsum(
        "hqk,qhd->khd",
        attn_probs.astype(jnp.bfloat16),
        grad_heads,
        preferred_element_type=jnp.float32,
    )
    value_grad = value_grad.reshape(key_rows.shape[0], -1).astype(jnp.bfloat16)
    return (key_grad, value_grad)


def spread(block, axis):
    size = lax.axis_size(axis)
    return lax.all_to_all(jnp.broadcast_to(block[None], (size,) + block.shape), axis, 0, 0)


def share_sum(blocks, axis):
    return jnp.sum(lax.all_to_all(blocks, axis, 0, 0).astype(jnp.float32), axis=0)


def swap(block):
    return lax.ppermute(block, "segment", [(0, 1), (1, 0)])


def to_chunks(block, parts):
    high, wide = (block.shape[0] // 8, block.shape[1] // 128)
    tiles = block.reshape(high, 8, wide, 128).transpose(0, 2, 1, 3).reshape(-1, 8, 128)
    each = -(-tiles.shape[0] // parts)
    tiles = jnp.pad(tiles, ((0, each * parts - tiles.shape[0]), (0, 0), (0, 0)))
    return tiles.reshape(parts, each, 8, 128)


def from_chunks(chunks, rows, cols):
    high, wide = (rows // 8, cols // 128)
    tiles = chunks.reshape(-1, 8, 128)[: high * wide]
    return tiles.reshape(high, wide, 8, 128).transpose(0, 2, 1, 3).reshape(rows, cols)


def shards(
    frames, dec_states, out_grad, frame_lengths, token_lengths, weights, norm_gains, norm_biases
):
    core = lax.axis_index("segment")
    first = core == 0
    own = weights[0]
    shard_rows, features = frames.shape[1:]
    mp = lax.axis_size("mp")
    dp = lax.axis_size("dp")
    head_cols = own.shape[1]
    rows = shard_rows * mp
    half = features // 2

    def mine(array):
        return lax.dynamic_index_in_dim(array, core, 0, keepdims=False)

    inputs = mine(frames)
    tokens = mine(dec_states)
    upstream = mine(out_grad)
    frame_ids = utterance_ids(mine(frame_lengths)[0], rows)
    token_ids = utterance_ids(mine(token_lengths)[0], tokens.shape[0])
    out_sent = lax.ppermute(own[3, :, half:], "segment", [(0, 1)])
    out_part = jnp.where(first, own[3, :, :half], out_sent)
    out_part = lax.all_gather(out_part, "mp", axis=0, tiled=True)
    out_rest = swap(out_part)
    enc_full = spread(inputs, "mp").reshape(rows, features)
    other = swap(own)
    enc = jnp.where(first, own, other)
    dec = jnp.where(first, other, own)
    normed = layer_norm(enc_full.astype(jnp.float32), norm_gains[0], norm_biases[0]).astype(
        jnp.bfloat16
    )
    queries = project(normed, enc[0])
    key_rows = project(normed, enc[1])
    value_rows = project(normed, enc[2])
    context, probs = attend(queries, key_rows, value_rows, frame_ids[:, None] == frame_ids[None, :])
    context_full = spread(context, "mp").transpose(1, 0, 2).reshape(rows, mp * head_cols)
    out_mine = jnp.dot(context_full, out_part, preferred_element_type=jnp.float32)
    out_other = jnp.dot(context_full, out_rest, preferred_element_type=jnp.float32)
    summed = jnp.concatenate(
        [jnp.where(first, out_mine, out_other), jnp.where(first, out_other, out_mine)], axis=1
    )
    states_full = (enc_full.astype(jnp.float32) + summed).astype(jnp.bfloat16)
    states = lax.dynamic_slice_in_dim(states_full, lax.axis_index("mp") * shard_rows, shard_rows, 0)
    state_normed = layer_norm(
        states_full.astype(jnp.float32), norm_gains[2], norm_biases[2]
    ).astype(jnp.bfloat16)
    token_normed = layer_norm(tokens.astype(jnp.float32), norm_gains[1], norm_biases[1]).astype(
        jnp.bfloat16
    )
    dec_queries = project(token_normed, dec[0])
    dec_keys = project(state_normed, dec[1])
    dec_values = project(state_normed, dec[2])
    dec_context, dec_probs = attend(
        dec_queries, dec_keys, dec_values, token_ids[:, None] == frame_ids[None, :]
    )
    grad_context = project(upstream, dec[3])
    dec_key_grad, dec_value_grad = attend_backward(
        dec_queries, dec_keys, dec_values, dec_probs, grad_context
    )
    partial = (
        jnp.dot(dec_key_grad, dec[1], preferred_element_type=jnp.float32)
        + jnp.dot(dec_value_grad, dec[2], preferred_element_type=jnp.float32)
    ).astype(jnp.bfloat16)

    def combine(term):
        left, right = (term[:, :half], term[:, half:])
        sent = swap(jnp.where(first, right, left).astype(jnp.bfloat16))
        return (jnp.where(first, left, right) + sent.astype(jnp.float32)).astype(jnp.bfloat16)

    def reduce_groups(term):
        total = share_sum(to_chunks(term, dp), "dp").astype(jnp.bfloat16)
        return from_chunks(spread(total, "dp"), 3 * head_cols, half)

    dec_term = jnp.concatenate(
        [
            outer_rows(dec_key_grad, state_normed),
            outer_rows(dec_value_grad, state_normed),
            outer_rows(dec_context, upstream),
        ]
    )
    pieces = lax.all_to_all(partial.reshape(mp, shard_rows, features), "mp", 0, 0)
    pieces, dec_part = lax.optimization_barrier((pieces, combine(dec_term)))
    dec_total = lax.psum(dec_part, "dp")
    summed = jnp.sum(pieces.astype(jnp.float32), axis=0)
    grads = norm_backward(summed, states.astype(jnp.float32), norm_gains[2]).astype(jnp.bfloat16)
    grads_full = spread(grads, "mp").reshape(rows, features)
    att_grad = project(grads_full, enc[3])
    enc_key_grad, enc_value_grad = attend_backward(queries, key_rows, value_rows, probs, att_grad)
    enc_term = jnp.concatenate(
        [
            outer_rows(enc_key_grad, normed),
            outer_rows(enc_value_grad, normed),
            outer_rows(context, grads_full),
        ]
    )
    enc_total = reduce_groups(combine(enc_term))
    kept = jnp.where(first, enc_total, dec_total)
    got = swap(jnp.where(first, dec_total, enc_total))
    gradient = jnp.concatenate(
        [jnp.where(first, kept, got), jnp.where(first, got, kept)], axis=1
    ).astype(jnp.float32)
    return gradient.reshape(1, 3, head_cols, features)


def solution(mesh):
    placed = (
        P(None, ("dp", "mp"), None),
        P(None, "dp", None),
        P(None, "dp", None),
        P(None, "dp", None),
        P(None, "dp", None),
        P("segment", None, "mp", None),
        P(),
        P(),
    )
    return jax.shard_map(
        shards,
        mesh=mesh,
        in_specs=placed,
        out_specs=P("segment", None, "mp", None),
        check_vma=False,
    )
```

profile of v0, /device:TPU:1, one launch (start us, length us, event | category | flops | bytes accessed | tf_op | source)
XLA Modules:
  0.0 379.2 jit_solution(9192799755561751875)
XLA Ops:
  8.5 10.9 %all-to-all-start = ((bf16[8,32,1280]{2,1,0:T(8,128)(2,1)}), bf16[8,32,1280]{2,1,0:T(8,128)(2,1)S(1)}, u32[]{:S(2)}, u32[]{:S(2)}) async-start(bf16[8,32,1280]{2,1,0:T(8,128)(2,1)} %broadcast_in_dim.31), calls=%async_computation | async-start | bytes 1310720 | tf_op jit(solution)/shard_map/all_to_all | solution.py:104
  19.4 2.9 collective-permute-start
  27.3 12.8 %all-to-all-done = bf16[8,32,1280]{2,1,0:T(8,128)(2,1)S(1)} async-done(((bf16[8,32,1280]{2,1,0:T(8,128)(2,1)}), bf16[8,32,1280]{2,1,0:T(8,128)(2,1)S(1)}, u32[]{:S(2)}, u32[]{:S(2)}) %all-to-all-start) | async-done | bytes 655392 | tf_op jit(solution)/shard_map/all_to_all | solution.py:104
  41.4 1.5 broadcast_select_fusion.1
  44.4 23.2 %all-gather.2.cloned.1.call-done = bf16[1024,640]{1,0:T(8,128)(2,1)} async-done(((bf16[128,640]{1,0:T(8,128)(2,1)}), bf16[1024,640]{1,0:T(8,128)(2,1)}) %all-gather.2.cloned.1.call-update) | async-done | bytes 1310736 | tf_op jit(solution)/shard_map/all_gather | solution.py:152
  67.6 7.2 %collective-permute-start.2 = (bf16[1024,640]{1,0:T(8,128)(2,1)}, bf16[1024,640]{1,0:T(8,128)(2,1)}, u32[]{:S(2)}, u32[]{:S(2)}) collective-permute-start(bf16[1024,640]{1,0:T(8,128)(2,1)} %all-gather.2.cloned.1.call-done), channel_id=1, source_target_pairs={{0,8},{8,0},{1,9},{9,1},{2,10},{10,2},{3,11},{11,3},{4,12},{12,4},... | collective-permute-start | bytes 3932168 | tf_op jit(solution)/shard_map/ppermute | solution.py:112
  77.4 3.9 %all-to-all-start.1 = ((bf16[8,256,128]{1,2,0:T(8,128)(2,1)}), bf16[8,256,128]{1,2,0:T(8,128)(2,1)S(1)}, u32[]{:S(2)}, u32[]{:S(2)}) async-start(bf16[8,256,128]{1,2,0:T(8,128)(2,1)} %broadcast_in_dim.34), calls=%async_computation.1 | async-start | bytes 1048576 | tf_op jit(solution)/shard_map/all_to_all | solution.py:104
  83.4 1.4 copy.34
  85.7 1.4 copy.35
  87.1 12.2 %all-to-all-done.1 = bf16[8,256,128]{1,2,0:T(8,128)(2,1)S(1)} async-done(((bf16[8,256,128]{1,2,0:T(8,128)(2,1)}), bf16[8,256,128]{1,2,0:T(8,128)(2,1)S(1)}, u32[]{:S(2)}, u32[]{:S(2)}) %all-to-all-start.1) | async-done | bytes 524320 | tf_op jit(solution)/shard_map/all_to_all | solution.py:104
  99.3 1.9 fusion.72
  101.2 1.9 broadcast_select_fusion.7
  107.3 2.4 fusion.25
  111.0 1.3 fusion.17
  114.6 2.2 fusion.2
  116.8 3.5 all-to-all-start.2
  120.3 1.6 pad_maximum_fusion
  122.0 2.4 collective-permute-start.3
  126.9 14.1 %all-to-all-done.2 = bf16[8,32,1280]{2,1,0:T(8,128)(2,1)S(1)} async-done(((bf16[8,32,1280]{2,1,0:T(8,128)(2,1)}), bf16[8,32,1280]{2,1,0:T(8,128)(2,1)S(1)}, u32[]{:S(2)}, u32[]{:S(2)}) %all-to-all-start.2) | async-done | bytes 655392 | tf_op jit(solution)/shard_map/all_to_all | solution.py:210
  141.5 22.3 %all_to_all.30 = bf16[8,32,1280]{2,1,0:T(8,128)(2,1)S(1)} all-to-all(bf16[8,32,1280]{2,1,0:T(8,128)(2,1)S(1)} %broadcast_in_dim.37), channel_id=1, replica_groups=mesh['dp'=32,'segment'=2,'mp'=8] {'mp'}, dimensions={0} | all-to-all | bytes 1310720 | tf_op jit(solution)/shard_map/all_to_all | solution.py:104
  163.8 1.4 convolution_convert_fusion
  165.5 1.5 convolution_convert_fusion.7
  167.3 1.4 fusion.16
  169.5 3.2 collective-permute-start.4
  172.7 1.5 collective-permute-done.4
  174.4 23.2 %all_to_all.31 = bf16[32,8,8,128]{3,2,1,0:T(8,128)(2,1)S(1)} all-to-all(bf16[32,8,8,128]{3,2,1,0:T(8,128)(2,1)S(1)} %bitcast.176), channel_id=1, replica_groups=mesh['dp'=32,'segment'=2,'mp'=8] {'dp'}, dimensions={0} | all-to-all | bytes 1048576 | tf_op jit(solution)/shard_map/all_to_all | solution.py:108
  198.6 8.1 %all-to-all-start.5 = ((bf16[32,8,8,128]{3,2,1,0:T(8,128)(2,1)}), bf16[32,8,8,128]{3,2,1,0:T(8,128)(2,1)S(1)}, u32[]{:S(2)}, u32[]{:S(2)}) async-start(bf16[32,8,8,128]{3,2,1,0:T(8,128)(2,1)} %broadcast_in_dim.42), calls=%async_computation.5 | async-start | bytes 1048576 | tf_op jit(solution)/shard_map/all_to_all | solution.py:104
  207.5 13.3 %all-to-all-done.5 = bf16[32,8,8,128]{3,2,1,0:T(8,128)(2,1)S(1)} async-done(((bf16[32,8,8,128]{3,2,1,0:T(8,128)(2,1)}), bf16[32,8,8,128]{3,2,1,0:T(8,128)(2,1)S(1)}, u32[]{:S(2)}, u32[]{:S(2)}) %all-to-all-start.5) | async-done | bytes 524320 | tf_op jit(solution)/shard_map/all_to_all | solution.py:104
  220.8 140.2 %all-reduce.3.cloned.1.call-done = bf16[384,640]{1,0:T(8,128)(2,1)} async-done(((bf16[384,640]{1,0:T(8,128)(2,1)}), bf16[384,640]{1,0:T(8,128)(2,1)}) %all-reduce.3.cloned.1.call-update) | async-done | bytes 491536 | tf_op jit(solution)/shard_map/psum | solution.py:212
  361.1 8.2 %collective-permute-start.5 = (bf16[384,640]{1,0:T(8,128)(2,1)S(1)}, bf16[384,640]{1,0:T(8,128)(2,1)S(1)}, u32[]{:S(2)}, u32[]{:S(2)}) collective-permute-start(bf16[384,640]{1,0:T(8,128)(2,1)S(1)} %broadcast_select_fusion.4), channel_id=1, source_target_pairs={{0,8},{8,0},{1,9},{9,1},{2,10},{10,2},{3,11},{11,3},{4,12},{12,4},... | collective-permute-start | bytes 1474568 | tf_op jit(solution)/shard_map/ppermute | solution.py:112
  369.3 1.5 collective-permute-done.5
  370.9 1.4 maximum_convert_fusion
  (142 shorter events, 29.2 us)
Async XLA Ops:
  6.5 78.3 %copy-start = (bf16[2,64,1280]{2,1,0:T(8,128)(2,1)S(1)}, bf16[2,64,1280]{2,1,0:T(8,128)(2,1)}, u32[]{:S(2)}) copy-start(bf16[2,64,1280]{2,1,0:T(8,128)(2,1)} %param.10) | copy-start | bytes 983044
  6.5 12.9 %copy-start.4 = (bf16[1,4,128,1280]{3,2,1,0:T(8,128)(2,1)S(1)}, bf16[1,4,128,1280]{3,2,1,0:T(8,128)(2,1)}, u32[]{:S(2)}) copy-start(bf16[1,4,128,1280]{3,2,1,0:T(8,128)(2,1)} %param.13) | copy-start | bytes 3932164
  6.5 17.1 %copy-start.20 = (s32[2,1,4]{2,1,0:T(1,128)S(1)}, s32[2,1,4]{2,1,0:T(1,128)}, u32[]{:S(2)}) copy-start(s32[2,1,4]{2,1,0:T(1,128)} %param.11) | copy-start | bytes 100
  6.5 17.1 %copy-start.21 = (s32[2,1,4]{2,1,0:T(1,128)S(1)}, s32[2,1,4]{2,1,0:T(1,128)}, u32[]{:S(2)}) copy-start(s32[2,1,4]{2,1,0:T(1,128)} %param.12) | copy-start | bytes 100
  6.5 17.4 %copy-start.8 = (bf16[2,64,1280]{2,1,0:T(8,128)(2,1)S(1)}, bf16[2,64,1280]{2,1,0:T(8,128)(2,1)}, u32[]{:S(2)}) copy-start(bf16[2,64,1280]{2,1,0:T(8,128)(2,1)} %param.9) | copy-start | bytes 983044
  7.6 18.3 %copy-start.14 = (f32[3,1280]{1,0:T(4,128)S(1)}, f32[3,1280]{1,0:T(4,128)}, u32[]{:S(2)}) copy-start(f32[3,1280]{1,0:T(4,128)} %param.15) | copy-start | bytes 46084
  7.6 18.3 %copy-start.15 = (f32[3,1280]{1,0:T(4,128)S(1)}, f32[3,1280]{1,0:T(4,128)}, u32[]{:S(2)}) copy-start(f32[3,1280]{1,0:T(4,128)} %param.14) | copy-start | bytes 46084
  8.5 31.6 %all-to-all-start = ((bf16[8,32,1280]{2,1,0:T(8,128)(2,1)}), bf16[8,32,1280]{2,1,0:T(8,128)(2,1)S(1)}, u32[]{:S(2)}, u32[]{:S(2)}) async-start(bf16[8,32,1280]{2,1,0:T(8,128)(2,1)} %broadcast_in_dim.31), calls=%async_computation | async-start | bytes 1310720 | tf_op jit(solution)/shard_map/all_to_all | solution.py:104
  19.3 48.2 %all-gather.2.cloned.1.call-start = ((), (), s32[]{:S(2)}) async-start(), calls=%async_computation.6 | async-start | bytes 1474560 | tf_op jit(solution)/shard_map/all_gather | solution.py:152
  19.4 21.6 %collective-permute-start = (bf16[4,128,1280]{2,1,0:T(8,128)(2,1)S(1)}, bf16[4,128,1280]{2,1,0:T(8,128)(2,1)}, u32[]{:S(2)}, u32[]{:S(2)}) collective-permute-start(bf16[4,128,1280]{2,1,0:T(8,128)(2,1)S(1)} %bitcast.177), channel_id=1, source_target_pairs={{0,8},{8,0},{1,9},{9,1},{2,10},{10,2},{3,11},{11,3},{4,12},{12,4},... | collective-permute-start | bytes 3932168 | tf_op jit(solution)/shard_map/ppermute | solution.py:112
  22.3 4.3 %collective-permute-start.1 = (bf16[128,640]{1,0:T(8,128)(2,1)S(1)}, bf16[128,640]{1,0:T(8,128)(2,1)S(1)}, u32[]{:S(2)}, u32[]{:S(2)}) collective-permute-start(bf16[128,640]{1,0:T(8,128)(2,1)S(1)} %slice_bitcast_fusion.18), channel_id=1, source_target_pairs={{0,8},{1,9},{2,10},{3,11},{4,12},{5,13},{6,14},{7,15},{16,24},{17,... | collective-permute-start | bytes 491528 | tf_op jit(solution)/shard_map/ppermute | solution.py:150
  24.0 1.9 copy-start.18
  25.3 50.7 %copy-start.10 = (pred[256,256]{0,1:T(8,128)(4,1)}, pred[256,256]{0,1:T(8,128)(4,1)S(1)}, u32[]{:S(2)}) copy-start(pred[256,256]{0,1:T(8,128)(4,1)S(1)} %broadcast_compare_fusion) | copy-start | bytes 196612
  42.9 41.9 %copy-start.2 = (bf16[4,128,1280]{2,1,0:T(8,128)(2,1)}, bf16[4,128,1280]{2,1,0:T(8,128)(2,1)S(1)}, u32[]{:S(2)}) copy-start(bf16[4,128,1280]{2,1,0:T(8,128)(2,1)S(1)} %get-tuple-element.22) | copy-start | bytes 3932164
  43.3 32.7 %copy-start.22 = (bf16[256,128]{0,1:T(8,128)(2,1)}, bf16[256,128]{0,1:T(8,128)(2,1)S(1)}, u32[]{:S(2)}) copy-start(bf16[256,128]{0,1:T(8,128)(2,1)S(1)} %convolution_convert_fusion.5) | copy-start | bytes 196612
  44.0 32.5 %copy-start.24 = (bf16[256,128]{0,1:T(8,128)(2,1)}, bf16[256,128]{0,1:T(8,128)(2,1)S(1)}, u32[]{:S(2)}) copy-start(bf16[256,128]{0,1:T(8,128)(2,1)S(1)} %convolution_convert_fusion.6) | copy-start | bytes 196612
  44.3 32.2 %copy-start.26 = (bf16[256,128]{0,1:T(8,128)(2,1)}, bf16[256,128]{0,1:T(8,128)(2,1)S(1)}, u32[]{:S(2)}) copy-start(bf16[256,128]{0,1:T(8,128)(2,1)S(1)} %convolution_convert_fusion.4) | copy-start | bytes 196612
  67.6 31.7 %collective-permute-start.2 = (bf16[1024,640]{1,0:T(8,128)(2,1)}, bf16[1024,640]{1,0:T(8,128)(2,1)}, u32[]{:S(2)}, u32[]{:S(2)}) collective-permute-start(bf16[1024,640]{1,0:T(8,128)(2,1)} %all-gather.2.cloned.1.call-done), channel_id=1, source_target_pairs={{0,8},{8,0},{1,9},{9,1},{2,10},{10,2},{3,11},{11,3},{4,12},{12,4},... | collective-permute-start | bytes 3932168 | tf_op jit(solution)/shard_map/ppermute | solution.py:112
  77.4 21.9 %all-to-all-start.1 = ((bf16[8,256,128]{1,2,0:T(8,128)(2,1)}), bf16[8,256,128]{1,2,0:T(8,128)(2,1)S(1)}, u32[]{:S(2)}, u32[]{:S(2)}) async-start(bf16[8,256,128]{1,2,0:T(8,128)(2,1)} %broadcast_in_dim.34), calls=%async_computation.1 | async-start | bytes 1048576 | tf_op jit(solution)/shard_map/all_to_all | solution.py:104
  104.0 1.7 copy-start.12
  112.4 2.2 copy-start.1
  116.8 24.2 %all-to-all-start.2 = ((bf16[8,32,1280]{2,1,0:T(8,128)(2,1)}), bf16[8,32,1280]{2,1,0:T(8,128)(2,1)S(1)}, u32[]{:S(2)}, u32[]{:S(2)}) async-start(bf16[8,32,1280]{2,1,0:T(8,128)(2,1)} %bitcast.37), calls=%async_computation.2 | async-start | bytes 1310720 | tf_op jit(solution)/shard_map/all_to_all | solution.py:210
  122.0 3.9 %collective-permute-start.3 = (bf16[384,640]{1,0:T(8,128)(2,1)S(1)}, bf16[384,640]{1,0:T(8,128)(2,1)S(1)}, u32[]{:S(2)}, u32[]{:S(2)}) collective-permute-start(bf16[384,640]{1,0:T(8,128)(2,1)S(1)} %select_convert_fusion.1), channel_id=1, source_target_pairs={{0,8},{8,0},{1,9},{9,1},{2,10},{10,2},{3,11},{11,3},{4,12},{12,4},... | collective-permute-start | bytes 1474568 | tf_op jit(solution)/shard_map/ppermute | solution.py:112
  163.8 1.7 copy-start.23
  163.8 1.7 copy-start.25
  163.8 1.7 copy-start.31
  165.4 1.5 copy-start.27
  169.5 4.7 %collective-permute-start.4 = (bf16[384,640]{1,0:T(8,128)(2,1)S(1)}, bf16[384,640]{1,0:T(8,128)(2,1)S(1)}, u32[]{:S(2)}, u32[]{:S(2)}) collective-permute-start(bf16[384,640]{1,0:T(8,128)(2,1)S(1)} %select_convert_fusion), channel_id=1, source_target_pairs={{0,8},{8,0},{1,9},{9,1},{2,10},{10,2},{3,11},{11,3},{4,12},{12,4},... | collective-permute-start | bytes 1474568 | tf_op jit(solution)/shard_map/ppermute | solution.py:112
  198.6 22.2 %all-to-all-start.5 = ((bf16[32,8,8,128]{3,2,1,0:T(8,128)(2,1)}), bf16[32,8,8,128]{3,2,1,0:T(8,128)(2,1)S(1)}, u32[]{:S(2)}, u32[]{:S(2)}) async-start(bf16[32,8,8,128]{3,2,1,0:T(8,128)(2,1)} %broadcast_in_dim.42), calls=%async_computation.5 | async-start | bytes 1048576 | tf_op jit(solution)/shard_map/all_to_all | solution.py:104
  206.7 154.3 %all-reduce.3.cloned.1.call-start = ((), (), s32[]{:S(2)}) async-start(), calls=%async_computation.7 | async-start | bytes 983040 | tf_op jit(solution)/shard_map/psum | solution.py:212
  361.0 9.8 %copy-start.6 = (bf16[384,640]{1,0:T(8,128)(2,1)S(1)}, bf16[384,640]{1,0:T(8,128)(2,1)}, u32[]{:S(2)}) copy-start(bf16[384,640]{1,0:T(8,128)(2,1)} %all-reduce.3.cloned.1.call-done) | copy-start | bytes 1474564
  361.1 9.7 %collective-permute-start.5 = (bf16[384,640]{1,0:T(8,128)(2,1)S(1)}, bf16[384,640]{1,0:T(8,128)(2,1)S(1)}, u32[]{:S(2)}, u32[]{:S(2)}) collective-permute-start(bf16[384,640]{1,0:T(8,128)(2,1)S(1)} %broadcast_select_fusion.4), channel_id=1, source_target_pairs={{0,8},{8,0},{1,9},{9,1},{2,10},{10,2},{3,11},{11,3},{4,12},{12,4},... | collective-permute-start | bytes 1474568 | tf_op jit(solution)/shard_map/ppermute | solution.py:112
  (12 other events, 15.6 us)
Sparse Core Ops, SparseCore 0:
  27.4 40.0 all-gather.1
  210.9 150.0 all-reduce.2
where the time goes:
time: 380 us; the launch traced here: 379 us
  waiting for transfers between devices  220 us (58%)
  starting transfers between devices  51.7 us (14%)
  blocking collectives  45.5 us (12%)
  matrix products  25.7 us (7%)
  between operations  14 us (4%)
  other arithmetic  13.8 us (4%)
  local copies, waits for them, and re-layouts  8.81 us (2%)
    psum x1, waiting for transfers between devices, shards(): dec_total = lax.psum(dec_part, 'dp')  140 us
    all_to_all x3, waiting for transfers between devices, spread(): lax.all_to_all(jnp.broadcast_to(block[None], (size,) + block.shape), axis...  38.3 us
    ppermute x5, starting transfers between devices, swap(): return lax.ppermute(block, 'segment', [(0, 1), (1, 0)])  23.9 us
    all_to_all x1, blocking collectives, share_sum(): lax.all_to_all(blocks, axis, 0, 0).astype(jnp.float32)  23.2 us
    all_gather x1, waiting for transfers between devices, shards(): out_part = lax.all_gather(out_part, 'mp', axis=0, tiled=True)  23.2 us
    all_to_all x3, starting transfers between devices, spread(): lax.all_to_all(jnp.broadcast_to(block[None], (size,) + block.shape), axis...  22.8 us
    all_to_all x1, blocking collectives, spread(): lax.all_to_all(jnp.broadcast_to(block[None], (size,) + block.shape), axis...  22.3 us
    all_to_all x1, waiting for transfers between devices, shards(): lax.all_to_all(partial.reshape(mp, shard_rows, features), 'mp', 0, 0)  14.1 us
  transfers between devices with their start and end apart: 12, of which 9 were waited for; matrix products, arithmetic and copies ran while one was open for 5% of the time, Pallas kernels for 0%

commit v1 on v0

--- a/solution.py
+++ b/solution.py
@@ -209,7 +209,7 @@
     )
     pieces = lax.all_to_all(partial.reshape(mp, shard_rows, features), "mp", 0, 0)
     pieces, dec_part = lax.optimization_barrier((pieces, combine(dec_term)))
-    dec_total = lax.psum(dec_part, "dp")
+    dec_total = lax.all_gather(dec_part, "dp").sum(axis=0)
     summed = jnp.sum(pieces.astype(jnp.float32), axis=0)
     grads = norm_backward(summed, states.astype(jnp.float32), norm_gains[2]).astype(jnp.bfloat16)
     grads_full = spread(grads, "mp").reshape(rows, features)

time: 380 us -> 312 us (0.82)
  waiting for transfers between devices: 220 us -> 124 us
  blocking collectives: 45.5 us -> 72.1 us
  starting transfers between devices: 51.7 us -> 40.5 us
  other arithmetic: 13.8 us -> 23.8 us
    psum x1 -> x0, waiting for transfers between devices: 140 us -> none  [shards(): dec_total = lax.psum(dec_part, 'dp')]
    all_gather x0 -> x1, waiting for transfers between devices: none -> 60.9 us  [shards(): dec_total = lax.all_gather(dec_part, 'dp').sum(axis=0)]
    all_to_all x1 -> x2, blocking collectives: 22.3 us -> 48.9 us  [spread(): lax.all_to_all(jnp.broadcast_to(block[None], (size,) + block.shape), axis...]
    all_to_all x3 -> x2, waiting for transfers between devices: 38.3 us -> 22.8 us  [spread(): lax.all_to_all(jnp.broadcast_to(block[None], (size,) + block.shape), axis...]
    reduce_sum x0 -> x1, other arithmetic: none -> 8.43 us  [shards(): dec_total = lax.all_gather(dec_part, 'dp').sum(axis=0)]
    all_to_all x3 -> x2, starting transfers between devices: 22.8 us -> 14.7 us  [spread(): lax.all_to_all(jnp.broadcast_to(block[None], (size,) + block.shape), axis...]
  transfers between devices with their start and end apart: 12 -> 11, of which waited for: 9 -> 8; matrix products, arithmetic and copies ran while one was open for 5% -> 9% of each run, Pallas kernels for 0% -> 0%
where the time goes in v1:
time: 312 us; the launch traced here: 311 us
  waiting for transfers between devices  124 us (40%)
  blocking collectives  72.1 us (23%)
  starting transfers between devices  40.5 us (13%)
  matrix products  28.9 us (9%)
  other arithmetic  23.8 us (8%)
  between operations  14 us (4%)
  local copies, waits for them, and re-layouts  7.94 us (3%)
    all_gather x1, waiting for transfers between devices, shards(): dec_total = lax.all_gather(dec_part, 'dp').sum(axis=0)  60.9 us
    all_to_all x2, blocking collectives, spread(): lax.all_to_all(jnp.broadcast_to(block[None], (size,) + block.shape), axis...  48.9 us
    all_to_all x1, blocking collectives, share_sum(): lax.all_to_all(blocks, axis, 0, 0).astype(jnp.float32)  23.2 us
    all_gather x1, waiting for transfers between devices, shards(): out_part = lax.all_gather(out_part, 'mp', axis=0, tiled=True)  23 us
    all_to_all x2, waiting for transfers between devices, spread(): lax.all_to_all(jnp.broadcast_to(block[None], (size,) + block.shape), axis...  22.8 us
    ppermute x5, starting transfers between devices, swap(): return lax.ppermute(block, 'segment', [(0, 1), (1, 0)])  20.2 us
    all_to_all x2, starting transfers between devices, spread(): lax.all_to_all(jnp.broadcast_to(block[None], (size,) + block.shape), axis...  14.7 us
    all_to_all x1, waiting for transfers between devices, shards(): lax.all_to_all(partial.reshape(mp, shard_rows, features), 'mp', 0, 0)  12.5 us
  transfers between devices with their start and end apart: 11, of which 8 were waited for; matrix products, arithmetic and copies ran while one was open for 9% of the time, Pallas kernels for 0%

profile of v1, /device:TPU:1, one launch (start us, length us, event | category | flops | bytes accessed | tf_op | source)
XLA Modules:
  0.0 310.9 jit_solution(10801803753165273172)
XLA Ops:
  8.5 10.9 %all-to-all-start = ((bf16[8,32,1280]{2,1,0:T(8,128)(2,1)}), bf16[8,32,1280]{2,1,0:T(8,128)(2,1)S(1)}, u32[]{:S(2)}, u32[]{:S(2)}) async-start(bf16[8,32,1280]{2,1,0:T(8,128)(2,1)} %broadcast_in_dim.31), calls=%async_computation | async-start | bytes 1310720 | tf_op jit(solution)/shard_map/all_to_all | solution.py:104
  19.4 2.9 collective-permute-start
  27.1 13.1 %all-to-all-done = bf16[8,32,1280]{2,1,0:T(8,128)(2,1)S(1)} async-done(((bf16[8,32,1280]{2,1,0:T(8,128)(2,1)}), bf16[8,32,1280]{2,1,0:T(8,128)(2,1)S(1)}, u32[]{:S(2)}, u32[]{:S(2)}) %all-to-all-start) | async-done | bytes 655392 | tf_op jit(solution)/shard_map/all_to_all | solution.py:104
  41.4 1.5 broadcast_select_fusion.1
  44.4 23.0 %all-gather.4.cloned.1.call-done = bf16[1024,640]{1,0:T(8,128)(2,1)} async-done(((bf16[128,640]{1,0:T(8,128)(2,1)}), bf16[1024,640]{1,0:T(8,128)(2,1)}) %all-gather.4.cloned.1.call-update) | async-done | bytes 1310736 | tf_op jit(solution)/shard_map/all_gather | solution.py:152
  67.3 7.2 %collective-permute-start.2 = (bf16[1024,640]{1,0:T(8,128)(2,1)}, bf16[1024,640]{1,0:T(8,128)(2,1)}, u32[]{:S(2)}, u32[]{:S(2)}) collective-permute-start(bf16[1024,640]{1,0:T(8,128)(2,1)} %all-gather.4.cloned.1.call-done), channel_id=1, source_target_pairs={{0,8},{8,0},{1,9},{9,1},{2,10},{10,2},{3,11},{11,3},{4,12},{12,4},... | collective-permute-start | bytes 3932168 | tf_op jit(solution)/shard_map/ppermute | solution.py:112
  77.1 3.9 %all-to-all-start.1 = ((bf16[8,256,128]{1,2,0:T(8,128)(2,1)}), bf16[8,256,128]{1,2,0:T(8,128)(2,1)S(1)}, u32[]{:S(2)}, u32[]{:S(2)}) async-start(bf16[8,256,128]{1,2,0:T(8,128)(2,1)} %broadcast_in_dim.34), calls=%async_computation.1 | async-start | bytes 1048576 | tf_op jit(solution)/shard_map/all_to_all | solution.py:104
  83.7 1.8 convolution_convert_fusion.11
  89.2 9.7 %all-to-all-done.1 = bf16[8,256,128]{1,2,0:T(8,128)(2,1)S(1)} async-done(((bf16[8,256,128]{1,2,0:T(8,128)(2,1)}), bf16[8,256,128]{1,2,0:T(8,128)(2,1)S(1)}, u32[]{:S(2)}, u32[]{:S(2)}) %all-to-all-start.1) | async-done | bytes 524320 | tf_op jit(solution)/shard_map/all_to_all | solution.py:104
  99.0 1.9 fusion.72
  100.9 1.9 broadcast_select_fusion.7
  106.0 2.2 fusion.74
  108.2 2.4 fusion.25
  113.3 2.3 fusion.73
  116.6 2.2 fusion.2
  118.8 4.2 %all-to-all-start.2 = ((bf16[8,32,1280]{2,1,0:T(8,128)(2,1)}), bf16[8,32,1280]{2,1,0:T(8,128)(2,1)}, u32[]{:S(2)}, u32[]{:S(2)}) async-start(bf16[8,32,1280]{2,1,0:T(8,128)(2,1)} %bitcast.176), calls=%async_computation.2 | async-start | bytes 1310720 | tf_op jit(solution)/shard_map/all_to_all | solution.py:210
  123.0 1.6 pad_maximum_fusion
  124.8 2.4 collective-permute-start.3
  127.1 1.5 collective-permute-done.3
  129.6 12.5 %all-to-all-done.2 = bf16[8,32,1280]{2,1,0:T(8,128)(2,1)} async-done(((bf16[8,32,1280]{2,1,0:T(8,128)(2,1)}), bf16[8,32,1280]{2,1,0:T(8,128)(2,1)}, u32[]{:S(2)}, u32[]{:S(2)}) %all-to-all-start.2) | async-done | bytes 655392 | tf_op jit(solution)/shard_map/all_to_all | solution.py:210
  144.2 21.0 %all_to_all.30 = bf16[8,32,1280]{2,1,0:T(8,128)(2,1)S(1)} all-to-all(bf16[8,32,1280]{2,1,0:T(8,128)(2,1)S(1)} %broadcast_in_dim.37), channel_id=1, replica_groups=mesh['dp'=32,'segment'=2,'mp'=8] {'mp'}, dimensions={0} | all-to-all | bytes 1310720 | tf_op jit(solution)/shard_map/all_to_all | solution.py:104
  166.6 1.5 convolution_convert_fusion.7
  168.3 1.4 fusion.16
  170.8 5.1 %collective-permute-start.4 = (bf16[384,640]{1,0:T(8,128)(2,1)S(1)}, bf16[384,640]{1,0:T(8,128)(2,1)S(1)}, u32[]{:S(2)}, u32[]{:S(2)}) collective-permute-start(bf16[384,640]{1,0:T(8,128)(2,1)S(1)} %select_convert_fusion), channel_id=1, source_target_pairs={{0,8},{8,0},{1,9},{9,1},{2,10},{10,2},{3,11},{11,3},{4,12},{12,4},... | collective-permute-start | bytes 1474568 | tf_op jit(solution)/shard_map/ppermute | solution.py:112
  176.0 1.5 collective-permute-done.4
  177.6 23.2 %all_to_all.31 = bf16[32,8,8,128]{3,2,1,0:T(8,128)(2,1)S(1)} all-to-all(bf16[32,8,8,128]{3,2,1,0:T(8,128)(2,1)S(1)} %bitcast.179), channel_id=1, replica_groups=mesh['dp'=32,'segment'=2,'mp'=8] {'dp'}, dimensions={0} | all-to-all | bytes 1048576 | tf_op jit(solution)/shard_map/all_to_all | solution.py:108
  201.0 27.9 %all_to_all.32 = bf16[32,8,8,128]{3,2,1,0:T(8,128)(2,1)S(1)} all-to-all(bf16[32,8,8,128]{3,2,1,0:T(8,128)(2,1)S(1)} %broadcast_in_dim.42), channel_id=1, replica_groups=mesh['dp'=32,'segment'=2,'mp'=8] {'dp'}, dimensions={0} | all-to-all | bytes 1048576 | tf_op jit(solution)/shard_map/all_to_all | solution.py:104
  229.0 60.9 %all-gather.6.cloned.1.call-done = bf16[12288,640]{1,0:T(8,128)(2,1)} async-done(((bf16[384,640]{1,0:T(8,128)(2,1)}), bf16[12288,640]{1,0:T(8,128)(2,1)}) %all-gather.6.cloned.1.call-update) | async-done | bytes 15728656 | tf_op jit(solution)/shard_map/all_gather | solution.py:212
  289.9 8.4 %reduce_sum.195 = bf16[384,640]{1,0:T(8,128)(2,1)S(1)} reduce(bf16[32,384,640]{2,1,0:T(8,128)(2,1)} %bitcast.160, bf16[]{:T(256)} %constant.67.clone.1), dimensions={0}, to_apply=%region_22.23 | reduce | flops 7618560 | bytes 16220162 | tf_op jit(solution)/shard_map/reduce_sum | solution.py:212
  298.4 2.6 collective-permute-start.5
  301.0 1.5 collective-permute-done.5
  302.6 1.4 maximum_convert_fusion
  (134 shorter events, 31.4 us)
Async XLA Ops:
  6.5 80.5 %copy-start = (bf16[2,64,1280]{2,1,0:T(8,128)(2,1)S(1)}, bf16[2,64,1280]{2,1,0:T(8,128)(2,1)}, u32[]{:S(2)}) copy-start(bf16[2,64,1280]{2,1,0:T(8,128)(2,1)} %param.10) | copy-start | bytes 983044
  6.5 12.9 %copy-start.5 = (bf16[1,4,128,1280]{3,2,1,0:T(8,128)(2,1)S(1)}, bf16[1,4,128,1280]{3,2,1,0:T(8,128)(2,1)}, u32[]{:S(2)}) copy-start(bf16[1,4,128,1280]{3,2,1,0:T(8,128)(2,1)} %param.13) | copy-start | bytes 3932164
  6.5 17.1 %copy-start.17 = (s32[2,1,4]{2,1,0:T(1,128)S(1)}, s32[2,1,4]{2,1,0:T(1,128)}, u32[]{:S(2)}) copy-start(s32[2,1,4]{2,1,0:T(1,128)} %param.11) | copy-start | bytes 100
  6.5 17.1 %copy-start.18 = (s32[2,1,4]{2,1,0:T(1,128)S(1)}, s32[2,1,4]{2,1,0:T(1,128)}, u32[]{:S(2)}) copy-start(s32[2,1,4]{2,1,0:T(1,128)} %param.12) | copy-start | bytes 100
  6.5 17.3 %copy-start.8 = (bf16[2,64,1280]{2,1,0:T(8,128)(2,1)S(1)}, bf16[2,64,1280]{2,1,0:T(8,128)(2,1)}, u32[]{:S(2)}) copy-start(bf16[2,64,1280]{2,1,0:T(8,128)(2,1)} %param.9) | copy-start | bytes 983044
  7.6 16.6 %copy-start.13 = (f32[3,1280]{1,0:T(4,128)S(1)}, f32[3,1280]{1,0:T(4,128)}, u32[]{:S(2)}) copy-start(f32[3,1280]{1,0:T(4,128)} %param.15) | copy-start | bytes 46084
  7.6 16.6 %copy-start.14 = (f32[3,1280]{1,0:T(4,128)S(1)}, f32[3,1280]{1,0:T(4,128)}, u32[]{:S(2)}) copy-start(f32[3,1280]{1,0:T(4,128)} %param.14) | copy-start | bytes 46084
  8.5 31.6 %all-to-all-start = ((bf16[8,32,1280]{2,1,0:T(8,128)(2,1)}), bf16[8,32,1280]{2,1,0:T(8,128)(2,1)S(1)}, u32[]{:S(2)}, u32[]{:S(2)}) async-start(bf16[8,32,1280]{2,1,0:T(8,128)(2,1)} %broadcast_in_dim.31), calls=%async_computation | async-start | bytes 1310720 | tf_op jit(solution)/shard_map/all_to_all | solution.py:104
  19.3 48.0 %all-gather.4.cloned.1.call-start = ((), (), s32[]{:S(2)}) async-start(), calls=%async_computation.6 | async-start | bytes 1474560 | tf_op jit(solution)/shard_map/all_gather | solution.py:152
  19.4 21.6 %collective-permute-start = (bf16[4,128,1280]{2,1,0:T(8,128)(2,1)S(1)}, bf16[4,128,1280]{2,1,0:T(8,128)(2,1)}, u32[]{:S(2)}, u32[]{:S(2)}) collective-permute-start(bf16[4,128,1280]{2,1,0:T(8,128)(2,1)S(1)} %bitcast.180), channel_id=1, source_target_pairs={{0,8},{8,0},{1,9},{9,1},{2,10},{10,2},{3,11},{11,3},{4,12},{12,4},... | collective-permute-start | bytes 3932168 | tf_op jit(solution)/shard_map/ppermute | solution.py:112
  22.3 4.1 %collective-permute-start.1 = (bf16[128,640]{1,0:T(8,128)(2,1)S(1)}, bf16[128,640]{1,0:T(8,128)(2,1)S(1)}, u32[]{:S(2)}, u32[]{:S(2)}) collective-permute-start(bf16[128,640]{1,0:T(8,128)(2,1)S(1)} %slice_bitcast_fusion.18), channel_id=1, source_target_pairs={{0,8},{1,9},{2,10},{3,11},{4,12},{5,13},{6,14},{7,15},{16,24},{17,... | collective-permute-start | bytes 491528 | tf_op jit(solution)/shard_map/ppermute | solution.py:150
  24.0 16.1 %copy-start.15 = (s32[256]{0:T(256)}, s32[256]{0:T(256)S(1)}, u32[]{:S(2)}) copy-start(s32[256]{0:T(256)S(1)} %convert_reduce_fusion.5) | copy-start | bytes 3076
  24.0 16.9 %copy-start.16 = (f32[64]{0:T(128)}, f32[64]{0:T(128)S(1)}, u32[]{:S(2)}) copy-start(f32[64]{0:T(128)S(1)} %broadcast_multiply_fusion.2) | copy-start | bytes 772
  24.2 51.6 %copy-start.9 = (pred[256,256]{0,1:T(8,128)(4,1)}, pred[256,256]{0,1:T(8,128)(4,1)S(1)}, u32[]{:S(2)}) copy-start(pred[256,256]{0,1:T(8,128)(4,1)S(1)} %broadcast_compare_fusion) | copy-start | bytes 196612
  42.9 44.0 %copy-start.3 = (bf16[4,128,1280]{2,1,0:T(8,128)(2,1)}, bf16[4,128,1280]{2,1,0:T(8,128)(2,1)S(1)}, u32[]{:S(2)}) copy-start(bf16[4,128,1280]{2,1,0:T(8,128)(2,1)S(1)} %get-tuple-element.22) | copy-start | bytes 3932164
  43.3 32.4 %copy-start.19 = (bf16[256,128]{0,1:T(8,128)(2,1)}, bf16[256,128]{0,1:T(8,128)(2,1)S(1)}, u32[]{:S(2)}) copy-start(bf16[256,128]{0,1:T(8,128)(2,1)S(1)} %convolution_convert_fusion.5) | copy-start | bytes 196612
  44.0 32.3 %copy-start.21 = (bf16[256,128]{0,1:T(8,128)(2,1)}, bf16[256,128]{0,1:T(8,128)(2,1)S(1)}, u32[]{:S(2)}) copy-start(bf16[256,128]{0,1:T(8,128)(2,1)S(1)} %convolution_convert_fusion.6) | copy-start | bytes 196612
  44.3 31.9 %copy-start.23 = (bf16[256,128]{0,1:T(8,128)(2,1)}, bf16[256,128]{0,1:T(8,128)(2,1)S(1)}, u32[]{:S(2)}) copy-start(bf16[256,128]{0,1:T(8,128)(2,1)S(1)} %convolution_convert_fusion.4) | copy-start | bytes 196612
  67.3 31.7 %collective-permute-start.2 = (bf16[1024,640]{1,0:T(8,128)(2,1)}, bf16[1024,640]{1,0:T(8,128)(2,1)}, u32[]{:S(2)}, u32[]{:S(2)}) collective-permute-start(bf16[1024,640]{1,0:T(8,128)(2,1)} %all-gather.4.cloned.1.call-done), channel_id=1, source_target_pairs={{0,8},{8,0},{1,9},{9,1},{2,10},{10,2},{3,11},{11,3},{4,12},{12,4},... | collective-permute-start | bytes 3932168 | tf_op jit(solution)/shard_map/ppermute | solution.py:112
  77.1 21.9 %all-to-all-start.1 = ((bf16[8,256,128]{1,2,0:T(8,128)(2,1)}), bf16[8,256,128]{1,2,0:T(8,128)(2,1)S(1)}, u32[]{:S(2)}, u32[]{:S(2)}) async-start(bf16[8,256,128]{1,2,0:T(8,128)(2,1)} %broadcast_in_dim.34), calls=%async_computation.1 | async-start | bytes 1048576 | tf_op jit(solution)/shard_map/all_to_all | solution.py:104
  103.8 1.8 copy-start.11
  113.2 3.4 %copy-start.2 = (f32[256,1280]{1,0:T(8,128)S(1)}, f32[256,1280]{1,0:T(8,128)}, u32[]{:S(2)}) copy-start(f32[256,1280]{1,0:T(8,128)} %fusion.25) | copy-start | bytes 3932164
  118.8 23.3 %all-to-all-start.2 = ((bf16[8,32,1280]{2,1,0:T(8,128)(2,1)}), bf16[8,32,1280]{2,1,0:T(8,128)(2,1)}, u32[]{:S(2)}, u32[]{:S(2)}) async-start(bf16[8,32,1280]{2,1,0:T(8,128)(2,1)} %bitcast.176), calls=%async_computation.2 | async-start | bytes 1310720 | tf_op jit(solution)/shard_map/all_to_all | solution.py:210
  123.0 166.9 %all-gather.6.cloned.1.call-start = ((), (), s32[]{:S(2)}) async-start(), calls=%async_computation.7 | async-start | bytes 16220160 | tf_op jit(solution)/shard_map/all_gather | solution.py:212
  124.8 3.8 %collective-permute-start.3 = (bf16[384,640]{1,0:T(8,128)(2,1)S(1)}, bf16[384,640]{1,0:T(8,128)(2,1)S(1)}, u32[]{:S(2)}, u32[]{:S(2)}) collective-permute-start(bf16[384,640]{1,0:T(8,128)(2,1)S(1)} %select_convert_fusion.1), channel_id=1, source_target_pairs={{0,8},{8,0},{1,9},{9,1},{2,10},{10,2},{3,11},{11,3},{4,12},{12,4},... | collective-permute-start | bytes 1474568 | tf_op jit(solution)/shard_map/ppermute | solution.py:112
  144.2 22.4 %copy-start.20 = (bf16[256,128]{0,1:T(8,128)(2,1)S(1)}, bf16[256,128]{0,1:T(8,128)(2,1)}, u32[]{:S(2)}) copy-start(bf16[256,128]{0,1:T(8,128)(2,1)} %copy-done.19) | copy-start | bytes 196612
  144.2 22.4 %copy-start.22 = (bf16[256,128]{0,1:T(8,128)(2,1)S(1)}, bf16[256,128]{0,1:T(8,128)(2,1)}, u32[]{:S(2)}) copy-start(bf16[256,128]{0,1:T(8,128)(2,1)} %copy-done.21) | copy-start | bytes 196612
  144.2 22.4 %copy-start.27 = (f32[2,256]{1,0:T(2,128)S(1)}, f32[2,256]{1,0:T(2,128)}, u32[]{:S(2)}) copy-start(f32[2,256]{1,0:T(2,128)} %copy-done.26) | copy-start | bytes 6148
  166.5 1.5 copy-start.24
  166.5 1.5 copy-start.25
  170.8 6.6 %collective-permute-start.4 = (bf16[384,640]{1,0:T(8,128)(2,1)S(1)}, bf16[384,640]{1,0:T(8,128)(2,1)S(1)}, u32[]{:S(2)}, u32[]{:S(2)}) collective-permute-start(bf16[384,640]{1,0:T(8,128)(2,1)S(1)} %select_convert_fusion), channel_id=1, source_target_pairs={{0,8},{8,0},{1,9},{9,1},{2,10},{10,2},{3,11},{11,3},{4,12},{12,4},... | collective-permute-start | bytes 1474568 | tf_op jit(solution)/shard_map/ppermute | solution.py:112
  298.4 4.1 %collective-permute-start.5 = (bf16[384,640]{1,0:T(8,128)(2,1)S(1)}, bf16[384,640]{1,0:T(8,128)(2,1)S(1)}, u32[]{:S(2)}, u32[]{:S(2)}) collective-permute-start(bf16[384,640]{1,0:T(8,128)(2,1)S(1)} %broadcast_select_fusion.4), channel_id=1, source_target_pairs={{0,8},{8,0},{1,9},{9,1},{2,10},{10,2},{3,11},{11,3},{4,12},{12,4},... | collective-permute-start | bytes 1474568 | tf_op jit(solution)/shard_map/ppermute | solution.py:112
  (7 other events, 8.8 us)
Sparse Core Ops, SparseCore 0:
  27.2 40.0 all-gather.3
  142.2 147.6 all-gather.5
